TPU v7x, 256 devices: a whole 4x4x8 slice. The times are simulated.
256 devices in a mesh: seq: 128 (over x, z, y), mp: 2 (over core).
Axes of the slice: x: 4, y: 4, z: 8, core: 2. Of those that a mesh axis runs over, the one named last changes fastest.
Arguments:
- states: bfloat16 [32768, 768], P('seq'), may hold values from -24 to 24
- qkv_weight: bfloat16 [3, 768, 768], P(None, None, 'mp'), may hold values from -0.21875 to 0.21875
- out_weight: bfloat16 [768, 768], P('mp'), may hold values from -0.21875 to 0.21875
- up_weight: bfloat16 [768, 3072], P(None, 'mp'), may hold values from -0.21875 to 0.21875
- down_weight: bfloat16 [3072, 768], P('mp'), may hold values from -0.109375 to 0.109375
- attn_gain: float32 [768], replicated, may hold values from 0.5 to 1.5
- mlp_gain: float32 [768], replicated, may hold values from 0.5 to 1.5
- global_ids: int32 [2], replicated, may hold values from 0 to 511, as said below
- random_owner: int32 [2, 512, 6, 3], P('mp', 'seq'), may hold values from 0 to 127, all different within a row; in each aligned block of 24 rows (0 to 23, 24 to 47, ..., all dimensions but the last counted through in order) at most 2 rows name the same one
- random_local: int32 [2, 512, 6, 3], P('mp', 'seq'), may hold values from 0 to 3
Outputs:
- layer_out: bfloat16 [32768, 768], P('seq')
Inputs may be any that keep to these rules, and one draw needn't show every extreme that they name: `global_ids`: 2 different block numbers; the second is 511. The random key block is random_owner * 4 + random_local. For one query block and head the 3 owners differ. Within the rows of one device (aligned blocks of 4 * K rows over the first three dimensions, K the third dimension) no owner is named more than 2 times, a bound that some block reaches.
All inputs are finite; a program needn't handle non-finite values.
Results may differ from a plain program's by a relative error of at most 0.008.
The roundings to bfloat16 on the way count: a program that leaves them out, or rounds other values in their place, can miss the bound.
Values may be sent and summed in bfloat16 or wider, within the bound.
No kernel may reach another device: no remote copies, remote signals or barrier semaphores. Data moves between devices by JAX's collectives and lax.ppermute only.
A program may use at most 192 MiB of HBM per device.

v0:
```python
import jax
import jax.numpy as jnp
from jax import lax
from jax.sharding import Mesh
from jax.sharding import PartitionSpec as P

HD = 64
BS = 64
R = 3
G = 2
SEQ = ("seq_0", "seq_1", "seq_2")
EPSILON = 1e-05
NEGATIVE = -1e30


def from_root(value, axes, root):
    value = jnp.where(lax.axis_index(axes) == root, value, jnp.zeros_like(value))
    for axis in axes:
        value = lax.psum(value, axis)
    return value


def with_halo(cells, sides, width):
    for axis, dim in sides:
        count = lax.axis_size(axis)
        ends = count - 1
        head = lax.slice_in_dim(cells, 0, width, axis=dim)
        tail = lax.slice_in_dim(cells, cells.shape[dim] - width, cells.shape[dim], axis=dim)
        cells = jnp.concatenate(
            [
                lax.ppermute(tail, axis, [(i, (i + 1) % count) for i in range(ends)]),
                cells,
                lax.ppermute(head, axis, [((i + 1) % count, i) for i in range(ends)]),
            ],
            axis=dim,
        )
    return cells


def collected_together(value, axis):
    leaves = jax.tree.leaves(value)
    order = sorted(range(len(leaves)), key=lambda k: -leaves[k].size)
    width = (1, *leaves[order[0]].shape)[-1]
    lines = [
        jnp.pad(leaves[k].reshape(-1), (0, -leaves[k].size % width)).reshape(-1, width)
        for k in order
    ]
    both, at, found = (lax.all_gather(jnp.concatenate(lines), axis), 0, {})
    for k, line in zip(order, lines):
        share = both[:, at : at + len(line)].reshape(len(both), -1)
        found[k] = share[:, : leaves[k].size].reshape(-1, *leaves[k].shape)
        at += len(line)
    numbers = iter(range(len(leaves)))
    return jax.tree.map(lambda _: found[next(numbers)], value)


def joined_all(value, axes, combine):
    for axis in axes:
        pieces = collected_together(value, axis)
        value = jax.tree.map(lambda part: part[0], pieces)
        for k in range(1, lax.axis_size(axis)):
            value = combine(value, jax.tree.map(lambda part: part[k], pieces))
    return value


def from_everyone(value, axis):
    copies = jnp.broadcast_to(value, (lax.axis_size(axis), *value.shape))
    return lax.all_to_all(copies, axis, split_axis=0, concat_axis=0, tiled=True)


def taken_together(value, axis):
    return from_everyone(value, axis).sum(axis=0)


def layer_norm(inputs, scales):
    center = jnp.mean(inputs, axis=-1, keepdims=True)
    shifted = inputs - center
    spread = jnp.mean(shifted * shifted, axis=-1, keepdims=True)
    return shifted * lax.rsqrt(spread + EPSILON) * scales


def merge_partials(earlier, later):
    high_early, total_early, acc_early = earlier
    high_late, total_late, acc_late = later
    highest = jnp.maximum(high_early, high_late)
    factor_early = jnp.exp(high_early - highest)
    factor_late = jnp.exp(high_late - highest)
    total = total_early * factor_early + total_late * factor_late
    summed = acc_early * factor_early[..., None] + acc_late * factor_late[..., None]
    return (highest, total, summed)


def fetch_global(query_blocks, pair_blocks, owner, local_block):
    query_piece = lax.dynamic_index_in_dim(query_blocks, local_block, 0, keepdims=False)
    pair_piece = lax.dynamic_index_in_dim(pair_blocks, local_block, 0, keepdims=False)
    return (from_root(query_piece, SEQ, owner), from_root(pair_piece, SEQ, owner))


def shards(
    states,
    qkv_weight,
    out_weight,
    up_weight,
    down_weight,
    attn_gain,
    mlp_gain,
    global_ids,
    random_owner,
    random_local,
):
    tokens_here = states.shape[0]
    head_width = qkv_weight.shape[2]
    head_count = head_width // HD
    block_count = tokens_here // BS
    seq_count = lax.axis_size(SEQ)
    position = lax.axis_index(SEQ)
    first_block = position * block_count
    scaling = HD ** (-0.5)
    highest = lax.Precision.HIGHEST
    queries = jnp.dot(states, qkv_weight[0], preferred_element_type=jnp.float32).astype(
        jnp.bfloat16
    )
    query_blocks = queries.reshape(block_count, BS, head_count, HD)
    key_part = jnp.dot(states, qkv_weight[1], preferred_element_type=jnp.float32).astype(
        jnp.bfloat16
    )
    value_part = jnp.dot(states, qkv_weight[2], preferred_element_type=jnp.float32).astype(
        jnp.bfloat16
    )
    key_value = jnp.concatenate(
        [
            key_part.reshape(tokens_here, head_count, HD),
            value_part.reshape(tokens_here, head_count, HD),
        ],
        axis=2,
    )
    pair_blocks = key_value.reshape(block_count, BS, head_count, 2 * HD)
    owner_of = global_ids // block_count
    local_of = global_ids % block_count
    fetched = [
        fetch_global(query_blocks, pair_blocks, owner_of[number], local_of[number])
        for number in range(G)
    ]
    global_query = jnp.stack([item[0] for item in fetched])
    global_pair = jnp.stack([item[1] for item in fetched])
    padded = with_halo(key_value, ((SEQ, 0),), BS)
    padded = padded.reshape(block_count + 2, BS, head_count, 2 * HD)
    window = jnp.stack([padded[shift_by : shift_by + block_count] for shift_by in range(3)], axis=1)
    neighbour = (
        first_block
        + jnp.arange(block_count, dtype=jnp.int32)[:, None]
        + jnp.arange(-1, 2, dtype=jnp.int32)[None, :]
    )
    inside = (neighbour >= 0) & (neighbour < seq_count * block_count)
    score_window = (
        jnp.einsum(
            "bqhd,bwkhd->bhqwk", query_blocks, window[..., :HD], preferred_element_type=jnp.float32
        )
        * scaling
    )
    score_window = jnp.where(inside[:, None, None, :, None], score_window, NEGATIVE)
    score_global = (
        jnp.einsum(
            "bqhd,gkhd->bhqgk",
            query_blocks,
            global_pair[..., :HD],
            preferred_element_type=jnp.float32,
        )
        * scaling
    )
    owner_list = random_owner.reshape(-1)
    local_list = random_local.reshape(-1)
    item_count = owner_list.shape[0]
    capacity = max(2, item_count // seq_count + 1)
    slot_total = seq_count * capacity
    head_list = jnp.broadcast_to(
        jnp.arange(head_count, dtype=jnp.int32)[None, :, None], (block_count, head_count, R)
    ).reshape(-1)
    matches = (owner_list[:, None] == jnp.arange(seq_count, dtype=jnp.int32)[None, :]).astype(
        jnp.int32
    )
    slot_rank = jnp.sum((jnp.cumsum(matches, axis=0) - matches) * matches, axis=1)
    slot_index = owner_list * capacity + slot_rank
    block_table = pair_blocks.transpose(0, 2, 1, 3).reshape(block_count * head_count, BS, 2 * HD)
    wanted = (
        jnp.zeros((slot_total,), jnp.int32).at[slot_index].set(local_list * head_count + head_list)
    )
    wanted = wanted.reshape(seq_count, capacity)
    remote = lax.all_to_all(
        block_table[lax.all_to_all(wanted, SEQ, split_axis=0, concat_axis=0, tiled=True)],
        SEQ,
        split_axis=0,
        concat_axis=0,
        tiled=True,
    ).reshape(slot_total, BS, 2 * HD)[slot_index]
    remote = remote.reshape(block_count, head_count, R, BS, 2 * HD)
    score_random = (
        jnp.einsum(
            "bqhd,bhrkd->bhqrk", query_blocks, remote[..., :HD], preferred_element_type=jnp.float32
        )
        * scaling
    )
    joined = jnp.concatenate([score_window, score_random, score_global], axis=3)
    joined_shape = joined.shape
    flat_scores = joined.reshape(joined_shape[0], joined_shape[1], joined_shape[2], -1)
    row_high = jnp.max(flat_scores, axis=-1, keepdims=True)
    raised = jnp.exp(flat_scores - row_high)
    weights = (
        (raised / jnp.sum(raised, axis=-1, keepdims=True))
        .astype(jnp.bfloat16)
        .reshape(joined_shape)
    )
    mixed = jnp.einsum(
        "bhqwk,bwkhd->bqhd",
        weights[:, :, :, :3],
        window[..., HD:],
        preferred_element_type=jnp.float32,
    )
    mixed = mixed + jnp.einsum(
        "bhqrk,bhrkd->bqhd",
        weights[:, :, :, 3 : 3 + R],
        remote[..., HD:],
        preferred_element_type=jnp.float32,
    )
    mixed = mixed + jnp.einsum(
        "bhqgk,gkhd->bqhd",
        weights[:, :, :, 3 + R :],
        global_pair[..., HD:],
        preferred_element_type=jnp.float32,
    )
    global_scores = (
        jnp.einsum(
            "gqhd,khd->hgqk",
            global_query,
            key_part.reshape(tokens_here, head_count, HD),
            preferred_element_type=jnp.float32,
        )
        * scaling
    )
    local_high = jnp.max(global_scores, axis=-1)
    global_raised = jnp.exp(global_scores - local_high[..., None])
    local_total = jnp.sum(global_raised, axis=-1)
    local_acc = jnp.einsum(
        "hgqk,khd->hgqd",
        global_raised,
        value_part.reshape(tokens_here, head_count, HD).astype(jnp.float32),
        precision=highest,
    )
    merged_high, merged_total, merged_acc = joined_all(
        (local_high, local_total, local_acc), SEQ, merge_partials
    )
    global_out = merged_acc / merged_total[..., None]
    placed_here = (
        global_ids[:, None] == first_block + jnp.arange(block_count, dtype=jnp.int32)[None, :]
    ).astype(jnp.float32)
    keep_rows = 1.0 - jnp.sum(placed_here, axis=0)
    placed = jnp.einsum("gb,hgqd->bqhd", placed_here, global_out, precision=highest)
    attended = (
        (mixed * keep_rows[:, None, None, None] + placed)
        .astype(jnp.bfloat16)
        .reshape(tokens_here, head_width)
    )
    projected = taken_together(
        jnp.dot(attended, out_weight, preferred_element_type=jnp.float32), "mp"
    )
    normed = layer_norm(states.astype(jnp.float32) + projected, attn_gain).astype(jnp.bfloat16)
    hidden = jax.nn.gelu(
        jnp.dot(normed, up_weight, preferred_element_type=jnp.float32), approximate=False
    ).astype(jnp.bfloat16)
    expanded = taken_together(
        jnp.dot(hidden, down_weight, preferred_element_type=jnp.float32), "mp"
    )
    return layer_norm(normed.astype(jnp.float32) + expanded, mlp_gain).astype(jnp.bfloat16)


def solution(mesh):
    split = Mesh(mesh.devices.reshape(4, 8, 4, mesh.shape["mp"]), ("seq_0", "seq_1", "seq_2", "mp"))
    placed = (
        P(SEQ, None),
        P(None, None, "mp"),
        P("mp", None),
        P(None, "mp"),
        P("mp", None),
        P(),
        P(),
        P(),
        P("mp", SEQ, None, None),
        P("mp", SEQ, None, None),
    )
    return jax.shard_map(
        shards, mesh=split, in_specs=placed, out_specs=P(SEQ, None), check_vma=False
    )
```

profile of v0, /device:TPU:1, one launch (start us, length us, event | category | flops | bytes accessed | tf_op | source)
XLA Modules:
  0.0 507.3 jit_solution(957818700047756081)
XLA Ops:
  6.5 0.8 broadcast_multiply_fusion.1
  7.4 0.8 copy.281
  9.9 0.8 scatter_custom_fusion
  11.5 16.9 %all-to-all-start = ((s32[128,1,2]{2,1,0:T(1,128)}), s32[128,1,2]{2,1,0:T(1,128)}, u32[]{:S(2)}, u32[]{:S(2)}) async-start(s32[128,1,2]{2,1,0:T(1,128)} %bitcast.15), calls=%async_computation | async-start | bytes 131072 | tf_op jit(solution)/shard_map/all_to_all | solution.py:190
  32.5 1.6 convolution_convert_fusion
  38.2 2.1 convolution_convert_fusion.2
  40.3 2.1 convolution_convert_fusion.1
  42.4 2.0 reshape.968
  44.4 1.1 copy.278
  45.6 2.1 reshape.969
  47.6 1.1 copy.279
  48.8 35.2 %all-reduce.21.cloned.1.call-done = (bf16[64,6,64]{2,0,1:T(8,128)(2,1)}, bf16[64,6,64]{2,0,1:T(8,128)(2,1)}) async-done(((bf16[64,6,64]{2,0,1:T(8,128)(2,1)}, bf16[64,6,64]{2,0,1:T(8,128)(2,1)}), (bf16[64,6,64]{2,0,1:T(8,128)(2,1)}, bf16[64,6,64]{2,0,1:T(8,128)(2,1)})) %all-reduce.21.cloned.1.call-update) | async-done | bytes 98320 | tf_op jit(solution)/shard_map/psum | solution.py:19
  84.1 0.8 fusion.82
  85.2 0.8 compare_select_fusion
  86.2 70.2 %all-reduce.13.cloned.1.call-done = (bf16[64,6,64]{2,0,1:T(8,128)(2,1)}, bf16[64,6,64]{2,0,1:T(8,128)(2,1)}) async-done(((bf16[64,6,64]{2,0,1:T(8,128)(2,1)}, bf16[64,6,64]{2,0,1:T(8,128)(2,1)}), (bf16[64,6,64]{2,0,1:T(8,128)(2,1)}, bf16[64,6,64]{2,0,1:T(8,128)(2,1)})) %all-reduce.13.cloned.1.call-update) | async-done | bytes 98320 | tf_op jit(solution)/shard_map/psum | solution.py:19
  156.4 3.1 gather_fusion
  159.5 12.3 %all-to-all-start.1 = ((bf16[128,2,64,128]{3,2,1,0:T(8,128)(2,1)}), bf16[128,2,64,128]{3,2,1,0:T(8,128)(2,1)}, u32[]{:S(2)}, u32[]{:S(2)}) async-start(bf16[128,2,64,128]{3,2,1,0:T(8,128)(2,1)} %bitcast.514), calls=%async_computation.1 | async-start | bytes 8388608 | tf_op jit(solution)/shard_map/all_to_all | solution.py:189
  172.0 0.8 copy.265
  172.9 39.6 %all-reduce.23.cloned.1.call-done = (bf16[64,6,128]{2,0,1:T(8,128)(2,1)}, bf16[64,6,128]{2,0,1:T(8,128)(2,1)}) async-done(((bf16[64,6,128]{2,0,1:T(8,128)(2,1)}, bf16[64,6,128]{2,0,1:T(8,128)(2,1)}), (bf16[64,6,128]{2,0,1:T(8,128)(2,1)}, bf16[64,6,128]{2,0,1:T(8,128)(2,1)})) %all-reduce.23.cloned.1.call-update) | async-done | bytes 196624 | tf_op jit(solution)/shard_map/psum | solution.py:19
  212.6 51.9 %all-reduce.17.cloned.1.call-done = (bf16[1,64,6,64]{3,1,0,2:T(8,128)(2,1)}, bf16[1,64,6,64]{3,1,2,0:T(8,128)(2,1)}) async-done(((bf16[1,64,6,64]{3,1,0,2:T(8,128)(2,1)}, bf16[1,64,6,64]{3,1,2,0:T(8,128)(2,1)}), (bf16[1,64,6,64]{3,1,0,2:T(8,128)(2,1)}, bf16[1,64,6,64]{3,1,2,0:T(8,128)(2,1)})) %all-reduce.17.cloned.1.call-update) | async-done | bytes 98320 | tf_op jit(solution)/shard_map/psum | solution.py:19
  264.5 1.3 fusion.188
  266.3 2.3 fusion.27
  268.7 1.1 copy.297
  269.9 12.6 %all-gather.3 = f32[4,792,64]{1,2,0:T(8,128)S(1)} all-gather(f32[1,792,64]{1,2,0:T(8,128)S(1)} %maximum_bitcast_fusion), channel_id=2, replica_groups=mesh['seq_0'=4,'seq_1'=8,'seq_2'=4,'mp'=2] {'seq_0'}, dimensions={0}, use_global_device_ids=true | all-gather | bytes 1013760 | tf_op jit(solution)/shard_map/all_gather | solution.py:48
  283.1 0.8 copy.303
  284.0 0.8 copy.300
  286.0 50.0 %all-reduce.15.cloned.1.call-done = (bf16[64,6,128]{2,0,1:T(8,128)(2,1)}, bf16[64,6,128]{2,0,1:T(8,128)(2,1)}) async-done(((bf16[64,6,128]{2,0,1:T(8,128)(2,1)}, bf16[64,6,128]{2,0,1:T(8,128)(2,1)}), (bf16[64,6,128]{2,0,1:T(8,128)(2,1)}, bf16[64,6,128]{2,0,1:T(8,128)(2,1)})) %all-reduce.15.cloned.1.call-update) | async-done | bytes 196624 | tf_op jit(solution)/shard_map/psum | solution.py:19
  336.2 1.8 maximum_bitcast_fusion.1
  338.0 1.8 fusion.39
  339.8 3.8 collective-permute-start
  343.6 1.5 collective-permute-start.1
  345.1 1.2 reshape.967
  346.2 1.1 reshape.966
  347.6 2.0 copy.270
  349.7 1.9 copy.269
  353.4 2.4 pad_maximum_fusion.3
  355.8 1.2 copy.266
  357.0 0.9 copy.271
  358.0 1.6 pad_maximum_fusion
  360.6 1.9 fusion.181
  362.5 24.5 %all-reduce.19.cloned.1.call-done = (bf16[1,64,6,128]{3,1,0,2:T(8,128)(2,1)}, bf16[1,64,6,128]{3,1,2,0:T(8,128)(2,1)}) async-done(((bf16[1,64,6,128]{3,1,0,2:T(8,128)(2,1)}, bf16[1,64,6,128]{3,1,2,0:T(8,128)(2,1)}), (bf16[1,64,6,128]{3,1,0,2:T(8,128)(2,1)}, bf16[1,64,6,128]{3,1,2,0:T(8,128)(2,1)})) %all-reduce.19.cloned.1.call-update) | async-done | bytes 196624 | tf_op jit(solution)/shard_map/psum | solution.py:19
  387.0 3.2 fusion.189
  390.2 38.0 %all-gather.8.cloned.1.call-done = f32[8,792,64]{1,2,0:T(8,128)} async-done(((f32[1,792,64]{1,2,0:T(8,128)}), f32[8,792,64]{1,2,0:T(8,128)}) %all-gather.8.cloned.1.call-update) | async-done | bytes 1622032 | tf_op jit(solution)/shard_map/all_gather | solution.py:48
  428.3 1.2 fusion.182
  431.6 1.6 fusion.41
  433.3 11.9 %all-gather.5 = f32[4,792,64]{1,2,0:T(8,128)S(1)} all-gather(f32[1,792,64]{1,2,0:T(8,128)S(1)} %maximum_bitcast_fusion.2), channel_id=4, replica_groups=mesh['seq_0'=4,'seq_1'=8,'seq_2'=4,'mp'=2] {'seq_2'}, dimensions={0}, use_global_device_ids=true | all-gather | bytes 1013760 | tf_op jit(solution)/shard_map/all_gather | solution.py:48
  445.2 0.8 fusion.184
  446.0 1.9 squeeze.257
  447.9 1.9 squeeze.255
  449.9 1.9 squeeze.253
  451.8 1.0 squeeze.250
  453.7 3.7 fusion.34
  457.4 3.1 gather_fusion.1
  460.5 1.6 fusion.190
  462.8 1.3 fusion.1
  464.0 1.3 divide_convert_fusion
  465.4 1.1 convolution_bitcast_fusion.1
  466.6 1.1 fusion.16
  469.4 12.9 %all_to_all.27 = f32[2,256,768]{2,1,0:T(8,128)} all-to-all(f32[2,256,768]{2,1,0:T(8,128)S(1)} %broadcast_in_dim.24), channel_id=1, replica_groups=mesh['seq_0'=4,'seq_1'=8,'seq_2'=4,'mp'=2] {'mp'}, dimensions={0} | all-to-all | bytes 3145728 | tf_op jit(solution)/shard_map/all_to_all | solution.py:68
  482.3 1.6 reduce_sum.97
  485.1 6.2 %fusion.24 = f32[256,768]{1,0:T(8,128)S(1)} fusion(bf16[1536,768]{1,0:T(8,128)(2,1)S(1)} %copy-done, bf16[256,768]{1,0:T(8,128)(2,1)S(1)} %multiply_convert_fusion.1, bf16[768,1536]{1,0:T(8,128)(2,1)} %param.13), kind=kOutput, calls=%fused_computation.56 | convolution fusion | flops 1233518592 | bytes 5898240 | tf_op jit(solution)/shard_map/dot_general | solution.py:271
  491.5 5.7 %all_to_all.28 = f32[2,256,768]{2,1,0:T(8,128)} all-to-all(f32[2,256,768]{2,1,0:T(8,128)S(1)} %broadcast_in_dim.25), channel_id=1, replica_groups=mesh['seq_0'=4,'seq_1'=8,'seq_2'=4,'mp'=2] {'mp'}, dimensions={0} | all-to-all | bytes 3145728 | tf_op jit(solution)/shard_map/all_to_all | solution.py:68
  497.2 1.6 reduce_sum.100
  499.5 0.9 multiply_convert_fusion
  (193 shorter events, 19.2 us)
Async XLA Ops:
  6.5 478.6 %copy-start = (bf16[1536,768]{1,0:T(8,128)(2,1)S(1)}, bf16[1536,768]{1,0:T(8,128)(2,1)}, u32[]{:S(2)}) copy-start(bf16[1536,768]{1,0:T(8,128)(2,1)} %param.14) | copy-start | bytes 7077892
  9.9 21.9 %copy-start.26 = (s32[72]{0:T(128)}, s32[72]{0:T(128)S(1)}, u32[]{:S(2)}) copy-start(s32[72]{0:T(128)S(1)} %fusion.141) | copy-start | bytes 868
  11.5 73.7 %all-to-all-start = ((s32[128,1,2]{2,1,0:T(1,128)}), s32[128,1,2]{2,1,0:T(1,128)}, u32[]{:S(2)}, u32[]{:S(2)}) async-start(s32[128,1,2]{2,1,0:T(1,128)} %bitcast.15), calls=%async_computation | async-start | bytes 131072 | tf_op jit(solution)/shard_map/all_to_all | solution.py:190
  28.4 55.6 %all-reduce.21.cloned.1.call-start = ((), (), s32[]{:S(2)}) async-start(), calls=%async_computation.9 | async-start | bytes 393216 | tf_op jit(solution)/shard_map/psum | solution.py:19
  32.5 5.7 %copy-start.7 = (bf16[256,768]{1,0:T(8,128)(2,1)S(1)}, bf16[256,768]{1,0:T(8,128)(2,1)}, u32[]{:S(2)}) copy-start(bf16[256,768]{1,0:T(8,128)(2,1)} %param.10) | copy-start | bytes 1179652
  34.4 7.9 %copy-start.5 = (bf16[4,64,6,64]{1,0,3,2:T(4,128)(2,1)}, bf16[4,64,6,64]{1,0,3,2:T(4,128)(2,1)S(1)}, u32[]{:S(2)}) copy-start(bf16[4,64,6,64]{1,0,3,2:T(4,128)(2,1)S(1)} %reshape.908) | copy-start | bytes 589828
  36.0 6.4 %copy-start.11 = (bf16[4,64,6,64]{3,1,2,0:T(8,128)(2,1)}, bf16[4,64,6,64]{3,1,2,0:T(8,128)(2,1)S(1)}, u32[]{:S(2)}) copy-start(bf16[4,64,6,64]{3,1,2,0:T(8,128)(2,1)S(1)} %copy.275) | copy-start | bytes 589828
  38.1 118.3 %all-reduce.13.cloned.1.call-start = ((), (), s32[]{:S(2)}) async-start(), calls=%async_computation.5 | async-start | bytes 393216 | tf_op jit(solution)/shard_map/psum | solution.py:19
  84.0 128.5 %all-reduce.23.cloned.1.call-start = ((), (), s32[]{:S(2)}) async-start(), calls=%async_computation.10 | async-start | bytes 393216 | tf_op jit(solution)/shard_map/psum | solution.py:19
  84.9 179.6 %all-reduce.17.cloned.1.call-start = ((), (), s32[]{:S(2)}) async-start(), calls=%async_computation.7 | async-start | bytes 393216 | tf_op jit(solution)/shard_map/psum | solution.py:19
  159.5 12.3 %copy-start.13 = (bf16[256,384]{1,0:T(8,128)(2,1)S(1)}, bf16[256,384]{1,0:T(8,128)(2,1)}, u32[]{:S(2)}) copy-start(bf16[256,384]{1,0:T(8,128)(2,1)} %convolution_convert_fusion.2) | copy-start | bytes 589828
  159.5 12.5 %copy-start.15 = (bf16[256,384]{1,0:T(8,128)(2,1)S(1)}, bf16[256,384]{1,0:T(8,128)(2,1)}, u32[]{:S(2)}) copy-start(bf16[256,384]{1,0:T(8,128)(2,1)} %convolution_convert_fusion.1) | copy-start | bytes 589828
  159.5 297.9 %all-to-all-start.1 = ((bf16[128,2,64,128]{3,2,1,0:T(8,128)(2,1)}), bf16[128,2,64,128]{3,2,1,0:T(8,128)(2,1)}, u32[]{:S(2)}, u32[]{:S(2)}) async-start(bf16[128,2,64,128]{3,2,1,0:T(8,128)(2,1)} %bitcast.514), calls=%async_computation.1 | async-start | bytes 8388608 | tf_op jit(solution)/shard_map/all_to_all | solution.py:189
  171.8 164.2 %all-reduce.15.cloned.1.call-start = ((), (), s32[]{:S(2)}) async-start(), calls=%async_computation.6 | async-start | bytes 393216 | tf_op jit(solution)/shard_map/psum | solution.py:19
  212.5 174.5 %all-reduce.19.cloned.1.call-start = ((), (), s32[]{:S(2)}) async-start(), calls=%async_computation.8 | async-start | bytes 393216 | tf_op jit(solution)/shard_map/psum | solution.py:19
  336.0 92.2 %all-gather.8.cloned.1.call-start = ((), (), s32[]{:S(2)}) async-start(), calls=%async_computation.4 | async-start | bytes 2064384 | tf_op jit(solution)/shard_map/all_gather | solution.py:48
  336.2 8.9 %copy-start.16 = (bf16[256,384]{1,0:T(8,128)(2,1)S(1)}, bf16[256,384]{1,0:T(8,128)(2,1)}, u32[]{:S(2)}) copy-start(bf16[256,384]{1,0:T(8,128)(2,1)} %convolution_convert_fusion.1) | copy-start | bytes 589828
  336.2 10.0 %copy-start.14 = (bf16[256,384]{1,0:T(8,128)(2,1)S(1)}, bf16[256,384]{1,0:T(8,128)(2,1)}, u32[]{:S(2)}) copy-start(bf16[256,384]{1,0:T(8,128)(2,1)} %convolution_convert_fusion.2) | copy-start | bytes 589828
  336.2 11.1 %copy-start.6 = (bf16[4,64,6,64]{1,0,3,2:T(4,128)(2,1)S(1)}, bf16[4,64,6,64]{1,0,3,2:T(4,128)(2,1)}, u32[]{:S(2)}) copy-start(bf16[4,64,6,64]{1,0,3,2:T(4,128)(2,1)} %copy-done.5) | copy-start | bytes 589828
  339.8 13.6 %collective-permute-start = (bf16[64,6,128]{0,2,1:T(8,128)(2,1)}, bf16[64,6,128]{0,2,1:T(8,128)(2,1)}, u32[]{:S(2)}, u32[]{:S(2)}) collective-permute-start(bf16[64,6,128]{0,2,1:T(8,128)(2,1)} %get-tuple-element.74), channel_id=1, source_target_pairs={{0,2},{2,4},{4,6},{6,8},{8,10},{10,12},{12,14},{14,16},{16,18},{18... | collective-permute-start | bytes 294920 | tf_op jit(solution)/shard_map/ppermute | solution.py:31
  343.6 9.9 %collective-permute-start.1 = (bf16[64,6,128]{0,2,1:T(8,128)(2,1)}, bf16[64,6,128]{0,2,1:T(8,128)(2,1)}, u32[]{:S(2)}, u32[]{:S(2)}) collective-permute-start(bf16[64,6,128]{0,2,1:T(8,128)(2,1)} %get-tuple-element.75), channel_id=1, source_target_pairs={{2,0},{4,2},{6,4},{8,6},{10,8},{12,10},{14,12},{16,14},{18,16},{20... | collective-permute-start | bytes 294920 | tf_op jit(solution)/shard_map/ppermute | solution.py:33
  346.2 5.4 %copy-start.28 = (s32[2]{0:T(128)S(1)}, s32[2]{0:T(128)}, u32[]{:S(2)}) copy-start(s32[2]{0:T(128)} %param.17) | copy-start | bytes 28
  346.2 6.6 %copy-start.27 = (s32[72]{0:T(128)S(1)}, s32[72]{0:T(128)}, u32[]{:S(2)}) copy-start(s32[72]{0:T(128)} %copy-done.26) | copy-start | bytes 868
  347.6 39.4 %copy-start.10 = (bf16[4,64,6,64,1]{3,1,4,2,0:T(8,128)(2,1)}, bf16[4,64,6,64,1]{3,1,4,2,0:T(8,128)(2,1)S(1)}, u32[]{:S(2)}) copy-start(bf16[4,64,6,64,1]{3,1,4,2,0:T(8,128)(2,1)S(1)} %copy.333) | copy-start | bytes 589828
  351.6 4.2 copy-start.29
  358.0 1.6 copy-start.12
  359.5 1.0 copy-start.3
  359.6 1.0 copy-start.25
  460.5 1.6 copy-start.21
  460.5 1.8 copy-start.1
  460.5 2.2 copy-start.2
  465.4 1.3 copy-start.4
  466.6 1.1 copy-start.17
  466.6 1.1 copy-start.19
  466.6 1.2 copy-start.20
  466.6 1.2 copy-start.24
  467.8 1.1 copy-start.18
  482.3 1.6 copy-start.8
  484.0 1.0 copy-start.9
  484.0 1.0 copy-start.22
  498.8 0.7 copy-start.23
Sparse Core Ops, SparseCore 0:
  38.2 45.6 all-reduce.20
  86.5 69.8 all-reduce.12
  158.7 53.7 all-reduce.22
  214.8 49.6 all-reduce.16
  266.7 69.2 all-reduce.14
  338.3 48.6 all-reduce.18
  388.8 39.4 all-gather.7
where the time goes:
time: 509 us; the launch traced here: 507 us
  waiting for transfers between devices  310 us (61%)
  local copies, waits for them, and re-layouts  45.3 us (9%)
  blocking collectives  43.1 us (8%)
  starting transfers between devices  34.7 us (7%)
  matrix products  27.7 us (5%)
  other arithmetic  27.3 us (5%)
  between operations  19.6 us (4%)
    psum x6, waiting for transfers between devices, from_root(): value = lax.psum(value, axis)  271 us
    all_gather x1, waiting for transfers between devices, collected_together(): both, at, found = (lax.all_gather(jnp.concatenate(lines), axis), 0, {})  38 us
    all_gather x2, blocking collectives, collected_together(): both, at, found = (lax.all_gather(jnp.concatenate(lines), axis), 0, {})  24.5 us
    all_to_all x2, blocking collectives, from_everyone(): return lax.all_to_all(copies, axis, split_axis=0, concat_axis=0, tiled=True)  18.6 us
    all_to_all x1, starting transfers between devices, shards(): lax.all_to_all(wanted, SEQ, split_axis=0, concat_axis=0, tiled=True)  16.9 us
    concatenate x8, local copies, waits for them, and re-layouts, shards(): jnp.concatenate([key_part.reshape(tokens_here, head_count, HD), value_par...  12.6 us
    all_to_all x1, starting transfers between devices, shards(): lax.all_to_all(block_table[lax.all_to_all(wanted, SEQ, split_axis=0, conc...  12.3 us
  transfers between devices with their start and end apart: 11, of which 7 were waited for; matrix products, arithmetic and copies ran while one was open for 14% of the time, Pallas kernels for 0%

commit v1 on v0

--- a/solution.py
+++ b/solution.py
@@ -16,7 +16,7 @@
 def from_root(value, axes, root):
     value = jnp.where(lax.axis_index(axes) == root, value, jnp.zeros_like(value))
     for axis in axes:
-        value = lax.psum(value, axis)
+        value = jnp.sum(jax.lax.all_gather(value, axis), 0)
     return value
 
 

time: 509 us -> 461 us (0.906)
  waiting for transfers between devices: 310 us -> 0.03 us
  blocking collectives: 43.1 us -> 295 us
  other arithmetic: 27.3 us -> 37.3 us
  local copies, waits for them, and re-layouts: 45.3 us -> 50.6 us
    psum x6 -> x0, waiting for transfers between devices: 271 us -> none  [from_root(): value = lax.psum(value, axis)]
    all_gather x0 -> x12, blocking collectives: none -> 204 us  [from_root(): value = jnp.sum(jax.lax.all_gather(value, axis), 0)]
    all_to_all x2, blocking collectives: 18.6 us -> 64.5 us  [from_everyone(): return lax.all_to_all(copies, axis, split_axis=0, concat_axis=0, tiled=True)]
    all_gather x1, waiting for transfers between devices: 38 us -> 0.01 us  [collected_together(): both, at, found = (lax.all_gather(jnp.concatenate(lines), axis), 0, {})]
    reduce_sum x0 -> x12, other arithmetic: none -> 8.98 us  [from_root(): value = jnp.sum(jax.lax.all_gather(value, axis), 0)]
    concatenate x8 -> x7, local copies, waits for them, and re-layouts: 12.6 us -> 11 us  [shards(): jnp.concatenate([key_part.reshape(tokens_here, head_count, HD), value_par...]
  transfers between devices with their start and end apart: 11 -> 5, of which waited for: 7 -> 0; matrix products, arithmetic and copies ran while one was open for 14% -> 18% of each run, Pallas kernels for 0% -> 0%
where the time goes in v1:
time: 461 us; the launch traced here: 460 us
  blocking collectives  295 us (64%)
  local copies, waits for them, and re-layouts  50.6 us (11%)
  other arithmetic  37.3 us (8%)
  starting transfers between devices  32.8 us (7%)
  matrix products  24.9 us (5%)
  between operations  19.2 us (4%)
    all_gather x12, blocking collectives, from_root(): value = jnp.sum(jax.lax.all_gather(value, axis), 0)  204 us
    all_to_all x2, blocking collectives, from_everyone(): return lax.all_to_all(copies, axis, split_axis=0, concat_axis=0, tiled=True)  64.5 us
    all_gather x2, blocking collectives, collected_together(): both, at, found = (lax.all_gather(jnp.concatenate(lines), axis), 0, {})  26.5 us
    all_to_all x1, starting transfers between devices, shards(): lax.all_to_all(wanted, SEQ, split_axis=0, concat_axis=0, tiled=True)  16.9 us
    all_to_all x1, starting transfers between devices, shards(): lax.all_to_all(block_table[lax.all_to_all(wanted, SEQ, split_axis=0, conc...  11.5 us
    concatenate x7, local copies, waits for them, and re-layouts, shards(): jnp.concatenate([key_part.reshape(tokens_here, head_count, HD), value_par...  11 us
  transfers between devices with their start and end apart: 5, of which 0 were waited for; matrix products, arithmetic and copies ran while one was open for 18% of the time, Pallas kernels for 0%

profile of v1, /device:TPU:1, one launch (start us, length us, event | category | flops | bytes accessed | tf_op | source)
XLA Modules:
  0.0 459.5 jit_solution(5131605182700496279)
XLA Ops:
  11.5 16.9 %all-to-all-start = ((s32[128,1,2]{2,1,0:T(1,128)}), s32[128,1,2]{2,1,0:T(1,128)}, u32[]{:S(2)}, u32[]{:S(2)}) async-start(s32[128,1,2]{2,1,0:T(1,128)} %bitcast.15), calls=%async_computation | async-start | bytes 131072 | tf_op jit(solution)/shard_map/all_to_all | solution.py:190
  28.4 1.6 convolution_convert_fusion.2
  30.0 1.5 convolution_convert_fusion.1
  32.6 3.1 collective-permute-start
  35.7 1.3 collective-permute-start.1
  37.0 1.4 convolution_convert_fusion
  38.7 1.0 concatenate.43
  46.6 1.2 broadcast_select_fusion.3
  47.9 14.7 %all_gather.97 = bf16[4,64,6,64]{3,1,2,0:T(8,128)(2,1)S(1)} all-gather(bf16[1,64,6,64]{3,1,2,0:T(8,128)(2,1)S(1)} %copy.311), channel_id=1, replica_groups=mesh['seq_0'=4,'seq_1'=8,'seq_2'=4,'mp'=2] {'seq_0'}, dimensions={0}, use_global_device_ids=true | all-gather | bytes 245760 | tf_op jit(solution)/shard_map/all_gather | solution.py:19
  63.4 19.9 %all-gather.6 = bf16[512,6,64]{2,0,1:T(8,128)(2,1)S(1)} all-gather(bf16[64,6,64]{2,0,1:T(8,128)(2,1)} %reduce_sum.249), channel_id=8, replica_groups=mesh['seq_0'=4,'seq_1'=8,'seq_2'=4,'mp'=2] {'seq_1'}, dimensions={0}, use_global_device_ids=true | all-gather | bytes 442368 | tf_op jit(solution)/shard_map/all_gather | solution.py:19
  84.1 10.4 %all-gather.7 = bf16[256,6,64]{2,0,1:T(8,128)(2,1)S(1)} all-gather(bf16[64,6,64]{2,0,1:T(8,128)(2,1)} %reduce_sum.250), channel_id=9, replica_groups=mesh['seq_0'=4,'seq_1'=8,'seq_2'=4,'mp'=2] {'seq_2'}, dimensions={0}, use_global_device_ids=true | all-gather | bytes 245760 | tf_op jit(solution)/shard_map/all_gather | solution.py:19
  95.3 1.1 copy.308
  96.4 10.2 %all_gather.92 = bf16[4,64,6,64]{3,1,2,0:T(8,128)(2,1)S(1)} all-gather(bf16[1,64,6,64]{3,1,2,0:T(8,128)(2,1)S(1)} %copy.308), channel_id=1, replica_groups=mesh['seq_0'=4,'seq_1'=8,'seq_2'=4,'mp'=2] {'seq_0'}, dimensions={0}, use_global_device_ids=true | all-gather | bytes 245760 | tf_op jit(solution)/shard_map/all_gather | solution.py:19
  107.3 19.9 %all-gather.4 = bf16[512,6,64]{2,0,1:T(8,128)(2,1)S(1)} all-gather(bf16[64,6,64]{2,0,1:T(8,128)(2,1)} %reduce_sum.246), channel_id=6, replica_groups=mesh['seq_0'=4,'seq_1'=8,'seq_2'=4,'mp'=2] {'seq_1'}, dimensions={0}, use_global_device_ids=true | all-gather | bytes 442368 | tf_op jit(solution)/shard_map/all_gather | solution.py:19
  128.1 9.9 %all-gather.5 = bf16[256,6,64]{2,0,1:T(8,128)(2,1)S(1)} all-gather(bf16[64,6,64]{2,0,1:T(8,128)(2,1)} %reduce_sum.247), channel_id=7, replica_groups=mesh['seq_0'=4,'seq_1'=8,'seq_2'=4,'mp'=2] {'seq_2'}, dimensions={0}, use_global_device_ids=true | all-gather | bytes 245760 | tf_op jit(solution)/shard_map/all_gather | solution.py:19
  138.7 1.3 fusion.184
  141.0 1.3 reshape.903
  142.3 1.4 copy.316
  144.4 2.3 fusion.27
  146.6 1.1 copy.314
  147.8 1.9 constant_dynamic-update-slice_fusion
  150.5 1.4 copy.288
  153.0 3.1 gather_fusion
  156.1 11.5 %all-to-all-start.1 = ((bf16[128,2,64,128]{3,2,1,0:T(8,128)(2,1)}), bf16[128,2,64,128]{3,2,1,0:T(8,128)(2,1)}, u32[]{:S(2)}, u32[]{:S(2)}) async-start(bf16[128,2,64,128]{3,2,1,0:T(8,128)(2,1)} %bitcast.514), calls=%async_computation.1 | async-start | bytes 8388608 | tf_op jit(solution)/shard_map/all_to_all | solution.py:189
  167.6 15.3 %all-gather.11 = f32[4,792,64]{1,2,0:T(8,128)S(1)} all-gather(f32[1,792,64]{1,2,0:T(8,128)S(1)} %maximum_bitcast_fusion), channel_id=10, replica_groups=mesh['seq_0'=4,'seq_1'=8,'seq_2'=4,'mp'=2] {'seq_0'}, dimensions={0}, use_global_device_ids=true | all-gather | bytes 1013760 | tf_op jit(solution)/shard_map/all_gather | solution.py:48
  184.6 1.1 bitcast_maximum_fusion
  185.7 1.3 fusion.64
  187.8 2.1 reshape.963
  189.8 2.0 reshape.962
  191.9 1.0 copy.350
  192.9 1.9 broadcast_select_fusion.1
  194.8 1.2 copy.297
  195.9 13.9 %all_gather.87 = bf16[4,64,6,128]{3,1,2,0:T(8,128)(2,1)S(1)} all-gather(bf16[1,64,6,128]{3,1,2,0:T(8,128)(2,1)S(1)} %copy.297), channel_id=1, replica_groups=mesh['seq_0'=4,'seq_1'=8,'seq_2'=4,'mp'=2] {'seq_0'}, dimensions={0}, use_global_device_ids=true | all-gather | bytes 491520 | tf_op jit(solution)/shard_map/all_gather | solution.py:19
  210.6 48.3 %all-gather.2 = bf16[512,6,128]{2,0,1:T(8,128)(2,1)S(1)} all-gather(bf16[64,6,128]{2,0,1:T(8,128)(2,1)} %reduce_sum.241), channel_id=4, replica_groups=mesh['seq_0'=4,'seq_1'=8,'seq_2'=4,'mp'=2] {'seq_1'}, dimensions={0}, use_global_device_ids=true | all-gather | bytes 884736 | tf_op jit(solution)/shard_map/all_gather | solution.py:19
  259.7 14.9 %all-gather.3 = bf16[256,6,128]{2,0,1:T(8,128)(2,1)S(1)} all-gather(bf16[64,6,128]{2,0,1:T(8,128)(2,1)} %reduce_sum.242), channel_id=5, replica_groups=mesh['seq_0'=4,'seq_1'=8,'seq_2'=4,'mp'=2] {'seq_2'}, dimensions={0}, use_global_device_ids=true | all-gather | bytes 491520 | tf_op jit(solution)/shard_map/all_gather | solution.py:19
  275.3 1.2 copy.294
  276.5 10.7 %all_gather.82 = bf16[4,64,6,128]{3,1,2,0:T(8,128)(2,1)S(1)} all-gather(bf16[1,64,6,128]{3,1,2,0:T(8,128)(2,1)S(1)} %copy.294), channel_id=1, replica_groups=mesh['seq_0'=4,'seq_1'=8,'seq_2'=4,'mp'=2] {'seq_0'}, dimensions={0}, use_global_device_ids=true | all-gather | bytes 491520 | tf_op jit(solution)/shard_map/all_gather | solution.py:19
  287.9 20.4 %all-gather = bf16[512,6,128]{2,0,1:T(8,128)(2,1)S(1)} all-gather(bf16[64,6,128]{2,0,1:T(8,128)(2,1)} %reduce_sum.238), channel_id=2, replica_groups=mesh['seq_0'=4,'seq_1'=8,'seq_2'=4,'mp'=2] {'seq_1'}, dimensions={0}, use_global_device_ids=true | all-gather | bytes 884736 | tf_op jit(solution)/shard_map/all_gather | solution.py:19
  309.0 10.4 %all-gather.1 = bf16[256,6,128]{2,0,1:T(8,128)(2,1)S(1)} all-gather(bf16[64,6,128]{2,0,1:T(8,128)(2,1)} %reduce_sum.239), channel_id=3, replica_groups=mesh['seq_0'=4,'seq_1'=8,'seq_2'=4,'mp'=2] {'seq_2'}, dimensions={0}, use_global_device_ids=true | all-gather | bytes 491520 | tf_op jit(solution)/shard_map/all_gather | solution.py:19
  320.2 1.9 copy.280
  322.1 1.9 copy.279
  325.2 1.8 fusion.185
  327.6 1.4 pad_maximum_fusion.3
  330.2 1.5 pad_maximum_fusion
  332.7 2.4 fusion.177
  335.1 1.3 fusion.178
  338.6 1.6 fusion.43
  340.3 11.2 %all-gather.13 = f32[4,792,64]{1,2,0:T(8,128)S(1)} all-gather(f32[1,792,64]{1,2,0:T(8,128)S(1)} %maximum_bitcast_fusion.2), channel_id=12, replica_groups=mesh['seq_0'=4,'seq_1'=8,'seq_2'=4,'mp'=2] {'seq_2'}, dimensions={0}, use_global_device_ids=true | all-gather | bytes 1013760 | tf_op jit(solution)/shard_map/all_gather | solution.py:48
  352.3 2.0 squeeze.257
  354.2 1.9 squeeze.255
  356.2 1.9 squeeze.253
  358.1 1.0 squeeze.250
  360.0 3.7 fusion.34
  363.7 3.1 gather_fusion.1
  366.8 1.6 fusion.186
  369.0 1.3 fusion.1
  370.3 1.3 divide_convert_fusion
  371.7 1.1 convolution_bitcast_fusion.1
  372.9 1.1 fusion.16
  375.8 58.8 %all_to_all.27 = f32[2,256,768]{2,1,0:T(8,128)} all-to-all(f32[2,256,768]{2,1,0:T(8,128)S(1)} %broadcast_in_dim.24), channel_id=1, replica_groups=mesh['seq_0'=4,'seq_1'=8,'seq_2'=4,'mp'=2] {'mp'}, dimensions={0} | all-to-all | bytes 3145728 | tf_op jit(solution)/shard_map/all_to_all | solution.py:68
  434.6 1.6 reduce_sum.253
  437.4 6.2 %fusion.24 = f32[256,768]{1,0:T(8,128)S(1)} fusion(bf16[1536,768]{1,0:T(8,128)(2,1)S(1)} %copy-done, bf16[256,768]{1,0:T(8,128)(2,1)S(1)} %multiply_convert_fusion.1, bf16[768,1536]{1,0:T(8,128)(2,1)} %param.13), kind=kOutput, calls=%fused_computation.56 | convolution fusion | flops 1233518592 | bytes 5898240 | tf_op jit(solution)/shard_map/dot_general | solution.py:271
  443.8 5.7 %all_to_all.28 = f32[2,256,768]{2,1,0:T(8,128)} all-to-all(f32[2,256,768]{2,1,0:T(8,128)S(1)} %broadcast_in_dim.25), channel_id=1, replica_groups=mesh['seq_0'=4,'seq_1'=8,'seq_2'=4,'mp'=2] {'mp'}, dimensions={0} | all-to-all | bytes 3145728 | tf_op jit(solution)/shard_map/all_to_all | solution.py:68
  449.5 1.6 reduce_sum.256
  (208 shorter events, 36.3 us)
Async XLA Ops:
  6.5 430.9 %copy-start = (bf16[1536,768]{1,0:T(8,128)(2,1)S(1)}, bf16[1536,768]{1,0:T(8,128)(2,1)}, u32[]{:S(2)}) copy-start(bf16[1536,768]{1,0:T(8,128)(2,1)} %param.14) | copy-start | bytes 7077892
  6.5 23.4 %copy-start.11 = (bf16[256,768]{1,0:T(8,128)(2,1)S(1)}, bf16[256,768]{1,0:T(8,128)(2,1)}, u32[]{:S(2)}) copy-start(bf16[256,768]{1,0:T(8,128)(2,1)} %param.10) | copy-start | bytes 1179652
  9.9 1.6 copy-start.28
  11.5 140.5 %all-to-all-start = ((s32[128,1,2]{2,1,0:T(1,128)}), s32[128,1,2]{2,1,0:T(1,128)}, u32[]{:S(2)}, u32[]{:S(2)}) async-start(s32[128,1,2]{2,1,0:T(1,128)} %bitcast.15), calls=%async_computation | async-start | bytes 131072 | tf_op jit(solution)/shard_map/all_to_all | solution.py:190
  29.9 1.5 copy-start.19
  31.5 7.2 %copy-start.20 = (bf16[256,384]{1,0:T(8,128)(2,1)}, bf16[256,384]{1,0:T(8,128)(2,1)S(1)}, u32[]{:S(2)}) copy-start(bf16[256,384]{1,0:T(8,128)(2,1)S(1)} %convolution_convert_fusion.1) | copy-start | bytes 589828
  31.6 8.0 %copy-start.6 = (bf16[256,384]{0,1:T(8,128)(2,1)}, bf16[256,384]{0,1:T(8,128)(2,1)S(1)}, u32[]{:S(2)}) copy-start(bf16[256,384]{0,1:T(8,128)(2,1)S(1)} %copy.274) | copy-start | bytes 589828
  31.8 7.8 %copy-start.8 = (bf16[256,384]{0,1:T(8,128)(2,1)}, bf16[256,384]{0,1:T(8,128)(2,1)S(1)}, u32[]{:S(2)}) copy-start(bf16[256,384]{0,1:T(8,128)(2,1)S(1)} %copy.275) | copy-start | bytes 589828
  31.8 7.8 %copy-start.30 = (s32[2]{0:T(128)S(1)}, s32[2]{0:T(128)}, u32[]{:S(2)}) copy-start(s32[2]{0:T(128)} %param.17) | copy-start | bytes 28
  32.6 295.0 %collective-permute-start = (bf16[64,6,128]{0,2,1:T(8,128)(2,1)}, bf16[64,6,128]{0,2,1:T(8,128)(2,1)}, u32[]{:S(2)}, u32[]{:S(2)}) collective-permute-start(bf16[64,6,128]{0,2,1:T(8,128)(2,1)} %get-tuple-element.62), channel_id=1, source_target_pairs={{0,2},{2,4},{4,6},{6,8},{8,10},{10,12},{12,14},{14,16},{16,18},{18... | collective-permute-start | bytes 294920 | tf_op jit(solution)/shard_map/ppermute | solution.py:31
  35.7 291.9 %collective-permute-start.1 = (bf16[64,6,128]{0,2,1:T(8,128)(2,1)}, bf16[64,6,128]{0,2,1:T(8,128)(2,1)}, u32[]{:S(2)}, u32[]{:S(2)}) collective-permute-start(bf16[64,6,128]{0,2,1:T(8,128)(2,1)} %get-tuple-element.63), channel_id=1, source_target_pairs={{2,0},{4,2},{6,4},{8,6},{10,8},{12,10},{14,12},{16,14},{18,16},{20... | collective-permute-start | bytes 294920 | tf_op jit(solution)/shard_map/ppermute | solution.py:33
  156.1 207.6 %all-to-all-start.1 = ((bf16[128,2,64,128]{3,2,1,0:T(8,128)(2,1)}), bf16[128,2,64,128]{3,2,1,0:T(8,128)(2,1)}, u32[]{:S(2)}, u32[]{:S(2)}) async-start(bf16[128,2,64,128]{3,2,1,0:T(8,128)(2,1)} %bitcast.514), calls=%async_computation.1 | async-start | bytes 8388608 | tf_op jit(solution)/shard_map/all_to_all | solution.py:189
  167.6 167.5 %all-gather.16.cloned.1.call-start = ((), (), s32[]{:S(2)}) async-start(), calls=%async_computation.4 | async-start | bytes 2064384 | tf_op jit(solution)/shard_map/all_gather | solution.py:48
  183.0 0.9 copy-start.10
  187.0 5.9 %copy-start.5 = (bf16[4,64,6,128]{1,0,3,2:T(4,128)(2,1)S(1)}, bf16[4,64,6,128]{1,0,3,2:T(4,128)(2,1)}, u32[]{:S(2)}) copy-start(bf16[4,64,6,128]{1,0,3,2:T(4,128)(2,1)} %constant_dynamic-update-slice_fusion) | copy-start | bytes 1179652
  309.0 15.0 %copy-start.31 = (s32[2]{0:T(128)S(1)}, s32[2]{0:T(128)}, u32[]{:S(2)}) copy-start(s32[2]{0:T(128)} %param.17) | copy-start | bytes 28
  309.0 16.2 %copy-start.14 = (bf16[4,64,6,64,1]{3,1,4,2,0:T(8,128)(2,1)S(1)}, bf16[4,64,6,64,1]{3,1,4,2,0:T(8,128)(2,1)}, u32[]{:S(2)}) copy-start(bf16[4,64,6,64,1]{3,1,4,2,0:T(8,128)(2,1)} %copy.350) | copy-start | bytes 589828
  320.2 5.1 %copy-start.15 = (bf16[64,6,128]{2,0,1:T(8,128)(2,1)S(1)}, bf16[64,6,128]{2,0,1:T(8,128)(2,1)}, u32[]{:S(2)}) copy-start(bf16[64,6,128]{2,0,1:T(8,128)(2,1)} %reduce_sum.243) | copy-start | bytes 294916
  320.2 5.1 %copy-start.17 = (bf16[64,6,128]{2,0,1:T(8,128)(2,1)S(1)}, bf16[64,6,128]{2,0,1:T(8,128)(2,1)}, u32[]{:S(2)}) copy-start(bf16[64,6,128]{2,0,1:T(8,128)(2,1)} %reduce_sum.240) | copy-start | bytes 294916
  322.1 4.9 %copy-start.29 = (s32[72]{0:T(128)S(1)}, s32[72]{0:T(128)}, u32[]{:S(2)}) copy-start(s32[72]{0:T(128)} %copy-done.28) | copy-start | bytes 868
  322.1 5.5 %copy-start.7 = (bf16[256,384]{0,1:T(8,128)(2,1)S(1)}, bf16[256,384]{0,1:T(8,128)(2,1)}, u32[]{:S(2)}) copy-start(bf16[256,384]{0,1:T(8,128)(2,1)} %copy-done.6) | copy-start | bytes 589828
  322.1 5.5 %copy-start.9 = (bf16[256,384]{0,1:T(8,128)(2,1)S(1)}, bf16[256,384]{0,1:T(8,128)(2,1)}, u32[]{:S(2)}) copy-start(bf16[256,384]{0,1:T(8,128)(2,1)} %copy-done.8) | copy-start | bytes 589828
  324.0 3.6 copy-start.32
  331.7 1.0 copy-start.3
  331.7 1.0 copy-start.27
  366.8 1.7 copy-start.23
  366.8 1.8 copy-start.1
  366.8 2.2 copy-start.2
  371.6 1.3 copy-start.4
  372.9 1.1 copy-start.16
  372.9 1.1 copy-start.18
  372.9 1.2 copy-start.21
  372.9 1.2 copy-start.26
  374.2 1.1 copy-start.22
  434.6 1.6 copy-start.12
  436.2 1.0 copy-start.13
  436.2 1.0 copy-start.24
  451.0 0.7 copy-start.25
Sparse Core Ops, SparseCore 0:
  187.9 88.2 all-gather.15
